TPU v7x, 32 devices: a whole 2x2x4 slice. The times are simulated.
32 devices in a mesh: dp: 8 (over y, x, core), tensor: 4 (over z).
Axes of the slice: x: 2, y: 2, z: 4, core: 2. Of those that a mesh axis runs over, the one named last changes fastest.
Arguments:
- block_input: bfloat16 [4096, 1024], P(('dp', 'tensor')), may hold values from -6 to 6
- segment_ids: int32 [8, 512], P('dp'), may hold values from 0 to 3, never falling along the last dimension, each value on 1 to 256 neighbouring positions
- attention_norm_gain: float32 [1024], replicated, may hold values from 0.1 to 1.9
- w_qkv: bfloat16 [1024, 2048], P('dp', 'tensor'), may hold values from -0.1875 to 0.1875
- w_og: bfloat16 [1024, 1024], P('dp', 'tensor'), may hold values from -0.1875 to 0.1875
- w_beta: bfloat16 [1024, 4], P('dp', 'tensor'), may hold values from -0.1875 to 0.1875
- w_alpha: bfloat16 [1024, 4], P('dp', 'tensor'), may hold values from -0.1875 to 0.1875
- conv_weight: float32 [4, 2048], P(None, 'tensor'), may hold values from -3 to 3
- a_log: float32 [4], P('tensor'), may hold values from -6 to -1
- dt_bias: float32 [4], P('tensor'), may hold values from -2 to 1
- out_gain: float32 [256], replicated, may hold values from 0.1 to 1.9
- w_out: bfloat16 [1024, 1024], P('tensor', 'dp'), may hold values from -0.1875 to 0.1875
- ffn_gain: float32 [1024], replicated, may hold values from 0.1 to 1.9
- w_ffn_gate: bfloat16 [1024, 2816], P('dp', 'tensor'), may hold values from -0.1875 to 0.1875
- w_ffn_up: bfloat16 [1024, 2816], P('dp', 'tensor'), may hold values from -0.1875 to 0.1875
- w_ffn_down: bfloat16 [2816, 1024], P('tensor', 'dp'), may hold values from -0.109375 to 0.109375
- cotangent: bfloat16 [4096, 1024], P(('dp', 'tensor')), may hold values from -6 to 6
Outputs:
- block_output: bfloat16 [4096, 1024], P(('dp', 'tensor'))
- input_grad: float32 [4096, 1024], P(('dp', 'tensor'))
- attn_gain_grad: float32 [1024], replicated
- w_qkv_grad: float32 [1024, 2048], P('dp', 'tensor')
- w_og_grad: float32 [1024, 1024], P('dp', 'tensor')
- w_beta_grad: float32 [1024, 4], P('dp', 'tensor')
- w_alpha_grad: float32 [1024, 4], P('dp', 'tensor')
- conv_weight_grad: float32 [4, 2048], P(None, 'tensor')
- a_log_grad: float32 [4], P('tensor')
- dt_bias_grad: float32 [4], P('tensor')
- out_gain_grad: float32 [256], replicated
- w_out_grad: float32 [1024, 1024], P('tensor', 'dp')
- ffn_gain_grad: float32 [1024], replicated
- w_ffn_gate_grad: float32 [1024, 2816], P('dp', 'tensor')
- w_ffn_up_grad: float32 [1024, 2816], P('dp', 'tensor')
- w_ffn_down_grad: float32 [2816, 1024], P('tensor', 'dp')
Inputs may be any that keep to these rules, and one draw needn't show every extreme that they name: `segment_ids`: along each sequence the document ids never fall; each of the 4 documents covers 1 to 256 positions, and some document has exactly 256.
All inputs are finite; a program needn't handle non-finite values.
Results may differ from a plain program's by a relative error of at most 0.012.
Values may be sent and summed in bfloat16 or wider, within the bound.
A program may use at most 128 MiB of HBM per device.

v0:
```python
from functools import partial

import jax
import jax.numpy as jnp
from jax import lax
from jax.sharding import PartitionSpec as P

DK = 128
DV = 256
STRETCH = 64
LEN = 512


HIGHEST = lax.Precision.HIGHEST


def matmul(left, right):
    return jnp.dot(left, right, preferred_element_type=jnp.float32)


def contract(form, left, right):
    return jnp.einsum(form, left, right, precision=HIGHEST)


def short_conv(mixer_in, conv_weight, segment):
    taps = conv_weight.shape[0]
    total = conv_weight[taps - 1] * mixer_in
    for offset in range(1, taps):
        shifted = jnp.concatenate(
            [jnp.zeros((offset, mixer_in.shape[1]), mixer_in.dtype), mixer_in[:-offset]], 0
        )
        earlier = jnp.concatenate([jnp.full((offset,), -1, jnp.int32), segment[:-offset]], 0)
        same_doc = (earlier == segment).astype(mixer_in.dtype)
        total = total + conv_weight[taps - 1 - offset] * shifted * same_doc[:, None]
    return jax.nn.silu(total)


def split_heads(activated, heads):
    grouped = activated.reshape(activated.shape[0], heads, 2 * DK + DV)
    query = grouped[..., :DK]
    keys = grouped[..., DK : 2 * DK]
    values = grouped[..., 2 * DK :]
    query = query * lax.rsqrt(jnp.sum(query * query, -1, keepdims=True) + 1e-06) * DK ** (-0.5)
    keys = keys * lax.rsqrt(jnp.sum(keys * keys, -1, keepdims=True) + 1e-06)
    return (query, keys, values)


def gated_norm(output_heads, gate_in, out_gain):
    rows, heads = (output_heads.shape[0], output_heads.shape[1])
    gate_heads = gate_in.reshape(rows, heads, DV)
    normed = (
        output_heads
        * lax.rsqrt(jnp.mean(output_heads * output_heads, -1, keepdims=True) + 1e-05)
        * out_gain
    )
    return (normed * jax.nn.silu(gate_heads)).reshape(rows, heads * DV)


def unit_lower_inverse(lower):
    identity = jnp.eye(lower.shape[-1], dtype=lower.dtype)
    result = identity - lower
    power = lower
    span = 2
    while span < lower.shape[-1]:
        power = contract("hij,hjk->hik", power, power)
        result = contract("hij,hjk->hik", result, identity + power)
        span = span * 2
    return result


def delta_blocks(query, keys, values, strength, log_decay, segment):
    rows, heads = (query.shape[0], query.shape[1])
    blocks = rows // STRETCH

    def to_blocks(array):
        return jnp.swapaxes(array.reshape((blocks, STRETCH) + array.shape[1:]), 1, 2)

    seg_blocks = segment.reshape(blocks, STRETCH)
    before = jnp.concatenate([jnp.full((1,), -1, jnp.int32), seg_blocks[:-1, -1]], 0)
    cumulative = jnp.cumsum(to_blocks(log_decay), axis=-1)
    position = jnp.arange(STRETCH)
    inclusive = position[:, None] >= position[None, :]
    below = (position[:, None] > position[None, :]).astype(jnp.float32)

    def advance(state, inputs):
        query_blk, key_blk, value_blk, strength_blk, cum_blk, seg_blk, seg_before = inputs
        keep = (seg_blk[:, None] == seg_blk[None, :]) & inclusive
        ratio = jnp.exp(
            jnp.where(keep, cum_blk[:, :, None] - cum_blk[:, None, :], 0.0)
        ) * keep.astype(jnp.float32)
        carry_in = jnp.exp(cum_blk) * (seg_blk == seg_before).astype(jnp.float32)
        lower = (
            strength_blk[:, :, None] * ratio * contract("htk,hjk->htj", key_blk, key_blk) * below
        )
        target = strength_blk[:, :, None] * (
            value_blk - carry_in[:, :, None] * contract("htk,hvk->htv", key_blk, state)
        )
        updates = contract("htj,hjv->htv", unit_lower_inverse(lower), target)
        weights = ratio * contract("htk,hjk->htj", query_blk, key_blk)
        output = carry_in[:, :, None] * contract("htk,hvk->htv", query_blk, state) + contract(
            "htj,hjv->htv", weights, updates
        )
        state = carry_in[:, -1][:, None, None] * state + contract(
            "hjv,hjk->hvk", updates * ratio[:, -1, :][:, :, None], key_blk
        )
        return (state, output)

    initial = jnp.zeros((heads, DV, DK), jnp.float32)
    _, output = lax.scan(
        advance,
        initial,
        (
            to_blocks(query),
            to_blocks(keys),
            to_blocks(values),
            to_blocks(strength),
            cumulative,
            seg_blocks,
            before,
        ),
    )
    return jnp.swapaxes(output, 1, 2).reshape(rows, heads, DV)


def mixer_core(
    segment, mixer_in, gate_in, beta_in, decay_in, conv_weight, a_log, dt_bias, out_gain
):
    heads = a_log.shape[0]
    query, keys, values = split_heads(short_conv(mixer_in, conv_weight, segment), heads)
    strength = jax.nn.sigmoid(beta_in)
    log_decay = -jnp.exp(a_log) * jax.nn.softplus(decay_in + dt_bias)
    output_heads = delta_blocks(query, keys, values, strength, log_decay, segment)
    return gated_norm(output_heads, gate_in, out_gain)


def root_mean_square_forward(rows):
    inverse_scale = lax.rsqrt(jnp.mean(rows * rows, -1, keepdims=True) + 1e-06)
    return (rows * inverse_scale, inverse_scale)


def root_mean_square_backward(normalized_input, inverse_scale, norm_gain, upstream_gradient):
    scaled_rows = upstream_gradient * norm_gain
    return (
        inverse_scale
        * (
            scaled_rows
            - normalized_input * jnp.mean(scaled_rows * normalized_input, -1, keepdims=True)
        ),
        jnp.sum(upstream_gradient * normalized_input, 0),
    )


def local(
    block_input,
    segment_ids,
    attention_norm_gain,
    w_qkv,
    w_og,
    w_beta,
    w_alpha,
    conv_weight,
    a_log,
    dt_bias,
    out_gain,
    w_out,
    ffn_gain,
    w_ffn_gate,
    w_ffn_up,
    w_ffn_down,
    cotangent,
):
    local_rows = block_input.shape[0]
    residual_input = block_input.astype(jnp.float32)
    attention_normalized_input, attention_scale = root_mean_square_forward(residual_input)
    local_normed_rows = (attention_normalized_input * attention_norm_gain).astype(jnp.bfloat16)
    full_qkv, full_og, full_beta, full_alpha, full_out = (
        lax.all_gather(w_qkv, "dp", axis=0, tiled=True),
        lax.all_gather(w_og, "dp", axis=0, tiled=True),
        lax.all_gather(w_beta, "dp", axis=0, tiled=True),
        lax.all_gather(w_alpha, "dp", axis=0, tiled=True),
        lax.all_gather(w_out, "dp", axis=1, tiled=True),
    )
    attention_normed = lax.all_gather(local_normed_rows, "tensor", axis=0, tiled=True)
    rows_all = attention_normed.shape[0]
    seq_count = rows_all // LEN
    mixer_in = matmul(attention_normed, full_qkv).reshape(seq_count, LEN, -1)
    gate_in = matmul(attention_normed, full_og).reshape(seq_count, LEN, -1)
    beta_in = matmul(attention_normed, full_beta).reshape(seq_count, LEN, -1)
    decay_in = matmul(attention_normed, full_alpha).reshape(seq_count, LEN, -1)
    core_all = jax.vmap(mixer_core, in_axes=(0, 0, 0, 0, 0, None, None, None, None))
    mixed_full, core_back = jax.vjp(
        partial(core_all, segment_ids),
        mixer_in,
        gate_in,
        beta_in,
        decay_in,
        conv_weight,
        a_log,
        dt_bias,
        out_gain,
    )
    mixed = mixed_full.reshape(rows_all, -1).astype(jnp.bfloat16)
    resid_mid = residual_input + lax.psum_scatter(
        matmul(lax.slice_in_dim(mixed, 0, lax.axis_size("tensor") * local_rows, axis=0), full_out),
        "tensor",
        scatter_dimension=0,
        tiled=True,
    )
    hhat, scale_ffn = root_mean_square_forward(resid_mid)
    normed_ffn_local = (hhat * ffn_gain).astype(jnp.bfloat16)
    full_fgate, full_fup, full_down = (
        lax.all_gather(w_ffn_gate, "dp", axis=0, tiled=True),
        lax.all_gather(w_ffn_up, "dp", axis=0, tiled=True),
        lax.all_gather(w_ffn_down, "dp", axis=1, tiled=True),
    )
    normed_ffn = lax.all_gather(normed_ffn_local, "tensor", axis=0, tiled=True)
    fgate = matmul(normed_ffn, full_fgate)
    fup = matmul(normed_ffn, full_fup)
    sigma = jax.nn.sigmoid(fgate)
    hidden = (fgate * sigma * fup).astype(jnp.bfloat16)
    block_output = (
        resid_mid
        + lax.psum_scatter(
            matmul(
                lax.slice_in_dim(hidden, 0, local_rows * lax.axis_size("tensor"), axis=0), full_down
            ).astype(jnp.bfloat16),
            "tensor",
            scatter_dimension=0,
            tiled=True,
        ).astype(jnp.float32)
    ).astype(jnp.bfloat16)
    grad_all = lax.all_gather(cotangent, "tensor", axis=0, tiled=True)
    dhidden = matmul(grad_all, full_down.T)
    dfgate = (dhidden * fup * sigma * (1.0 + fgate * (1.0 - sigma))).astype(jnp.bfloat16)
    dfup = (dhidden * fgate * sigma).astype(jnp.bfloat16)
    grad_down = matmul(hidden.T, grad_all)
    grad_fgate = matmul(normed_ffn.T, dfgate)
    grad_fup = matmul(normed_ffn.T, dfup)
    ffn_summed = (
        lax.psum_scatter(grad_fgate, "dp", scatter_dimension=0, tiled=True),
        lax.psum_scatter(grad_fup, "dp", scatter_dimension=0, tiled=True),
        lax.psum_scatter(grad_down, "dp", scatter_dimension=1, tiled=True),
    )
    gate_rows = lax.slice_in_dim(dfgate, 0, lax.axis_size("tensor") * local_rows, axis=0)
    up_rows = lax.slice_in_dim(dfup, 0, lax.axis_size("tensor") * local_rows, axis=0)
    dnormed_ffn = lax.psum_scatter(
        matmul(gate_rows, full_fgate.T) + matmul(up_rows, full_fup.T),
        "tensor",
        scatter_dimension=0,
        tiled=True,
    )
    dresid_norm, grad_ffn_gain = root_mean_square_backward(hhat, scale_ffn, ffn_gain, dnormed_ffn)
    dresid = cotangent.astype(jnp.float32) + dresid_norm
    dresid_b = dresid.astype(jnp.bfloat16)
    dresid_all = lax.all_gather(dresid_b, "tensor", axis=0, tiled=True)
    grad_out = matmul(mixed.T, dresid_all)
    dmixed = matmul(dresid_all, full_out.T).reshape(seq_count, LEN, -1)
    dmixer_f, dgate_f, dbeta_f, ddecay_f, grad_conv, grad_alog, grad_dt, grad_ogain = core_back(
        dmixed
    )
    dmixer_b = dmixer_f.reshape(rows_all, -1).astype(jnp.bfloat16)
    dgate_b = dgate_f.reshape(rows_all, -1).astype(jnp.bfloat16)
    dbeta_b = dbeta_f.reshape(rows_all, -1).astype(jnp.bfloat16)
    ddecay_b = ddecay_f.reshape(rows_all, -1).astype(jnp.bfloat16)
    grad_qkv = matmul(attention_normed.T, dmixer_b)
    grad_og = matmul(attention_normed.T, dgate_b)
    grad_beta = matmul(attention_normed.T, dbeta_b)
    grad_alpha = matmul(attention_normed.T, ddecay_b)
    total = matmul(dmixer_b, full_qkv.T)
    total = total + matmul(dgate_b, full_og.T)
    total = total + matmul(dbeta_b, full_beta.T)
    attention_normed_gradient = lax.psum_scatter(
        (total + matmul(ddecay_b, full_alpha.T)).astype(jnp.bfloat16),
        "tensor",
        scatter_dimension=0,
        tiled=True,
    ).astype(jnp.float32)
    norm_input_gradient, attention_gain_gradient = root_mean_square_backward(
        attention_normalized_input, attention_scale, attention_norm_gain, attention_normed_gradient
    )
    input_grad = dresid + norm_input_gradient
    mixer_summed = (
        lax.psum_scatter(grad_qkv, "dp", scatter_dimension=0, tiled=True),
        lax.psum_scatter(grad_og, "dp", scatter_dimension=0, tiled=True),
        lax.psum_scatter(grad_beta, "dp", scatter_dimension=0, tiled=True),
        lax.psum_scatter(grad_alpha, "dp", scatter_dimension=0, tiled=True),
        lax.psum_scatter(grad_out, "dp", scatter_dimension=1, tiled=True),
    )
    summed = mixer_summed + ffn_summed
    tensor_count = lax.axis_size("tensor")
    tensor_place = lax.axis_index("tensor")
    channels = conv_weight.shape[1]
    heads_here = a_log.shape[0]
    conv_full = lax.dynamic_update_slice_in_dim(
        jnp.zeros((conv_weight.shape[0], channels * tensor_count), jnp.float32),
        grad_conv,
        tensor_place * channels,
        1,
    )
    alog_full = lax.dynamic_update_slice_in_dim(
        jnp.zeros((heads_here * tensor_count,), jnp.float32),
        grad_alog,
        tensor_place * heads_here,
        0,
    )
    dt_full = lax.dynamic_update_slice_in_dim(
        jnp.zeros((heads_here * tensor_count,), jnp.float32), grad_dt, tensor_place * heads_here, 0
    )
    small = lax.psum(
        (attention_gain_gradient, grad_ffn_gain, grad_ogain, conv_full, alog_full, dt_full),
        ("dp", "tensor"),
    )
    attn_gain_grad, ffn_gain_grad, out_gain_grad, conv_total, alog_total, dt_total = small
    conv_weight_grad = lax.dynamic_slice_in_dim(conv_total, tensor_place * channels, channels, 1)
    a_log_grad = lax.dynamic_slice_in_dim(alog_total, tensor_place * heads_here, heads_here, 0)
    dt_bias_grad = lax.dynamic_slice_in_dim(dt_total, tensor_place * heads_here, heads_here, 0)
    return (
        block_output,
        input_grad,
        attn_gain_grad,
        summed[0],
        summed[1],
        summed[2],
        summed[3],
        conv_weight_grad,
        a_log_grad,
        dt_bias_grad,
        out_gain_grad,
        summed[4],
        ffn_gain_grad,
        summed[5],
        summed[6],
        summed[7],
    )


def solution(mesh):
    placed = (
        P(("dp", "tensor"), None),
        P("dp", None),
        P(),
        P("dp", "tensor"),
        P("dp", "tensor"),
        P("dp", "tensor"),
        P("dp", "tensor"),
        P(None, "tensor"),
        P("tensor"),
        P("tensor"),
        P(),
        P("tensor", "dp"),
        P(),
        P("dp", "tensor"),
        P("dp", "tensor"),
        P("tensor", "dp"),
        P(("dp", "tensor"), None),
    )
    return jax.shard_map(
        local,
        mesh=mesh,
        in_specs=placed,
        out_specs=(
            P(("dp", "tensor"), None),
            P(("dp", "tensor"), None),
            P(),
            P("dp", "tensor"),
            P("dp", "tensor"),
            P("dp", "tensor"),
            P("dp", "tensor"),
            P(None, "tensor"),
            P("tensor"),
            P("tensor"),
            P(),
            P("tensor", "dp"),
            P(),
            P("dp", "tensor"),
            P("dp", "tensor"),
            P("tensor", "dp"),
        ),
        check_vma=False,
    )
```

profile of v0, /device:TPU:0, one launch (start us, length us, event | category | flops | bytes accessed | tf_op | source)
XLA Modules:
  0.0 1323.6 jit_solution(17847353194612368250)
XLA Ops:
  15.5 10.4 all_gather.37
  25.8 8.6 all_gather.38
  34.5 10.8 all_gather.40
  45.3 11.3 all_gather.41
  60.5 6.3 all-gather.11.cloned.1.call-done
  77.8 189.3 %while.120 = (s32[]{:T(128)}, f32[1,1,256,128]{3,2,1,0:T(8,128)S(1)}, f32[8,1,1,64,256]{4,3,2,1,0:T(8,128)S(1)}, pred[8,1,1,64,64]{4,3,2,1,0:T(32,128)(4,1)S(1)}...) while((s32[]{:T(128)}, ...), condition=%wide.region_5.6_spmd.clone.clone, body=%wide.region_4.5_spmd.clone.clone.sunk | while | flops 145379904 | bytes 3605050 | solution.py:109
  273.0 43.2 %reduce-scatter.17.cloned.1.call-done = f32[128,1024]{1,0:T(8,128)} async-done(((f32[512,1024]{1,0:T(8,128)}), f32[128,1024]{1,0:T(8,128)}) %reduce-scatter.17.cloned.1.call-update) | async-done | bytes 524304 | tf_op jit(solution)/shard_map/reduce_scatter | solution.py:203
  320.5 21.8 %all-gather.15.cloned.1.call-done = bf16[1024,704]{0,1:T(8,128)(2,1)} async-done(((bf16[128,704]{0,1:T(8,128)(2,1)}), bf16[1024,704]{0,1:T(8,128)(2,1)}) %all-gather.15.cloned.1.call-update) | async-done | bytes 1441808 | tf_op jit(solution)/shard_map/all_gather | solution.py:212
  342.3 30.0 %all-gather.13.cloned.1.call-done = bf16[512,1024]{1,0:T(8,128)(2,1)} async-done(((bf16[128,1024]{1,0:T(8,128)(2,1)}), bf16[512,1024]{1,0:T(8,128)(2,1)}) %all-gather.13.cloned.1.call-update) | async-done | bytes 1048592 | tf_op jit(solution)/shard_map/all_gather | solution.py:216
  376.0 22.6 %all-gather.17.cloned.1.call-done = bf16[1024,704]{0,1:T(8,128)(2,1)} async-done(((bf16[128,704]{0,1:T(8,128)(2,1)}), bf16[1024,704]{0,1:T(8,128)(2,1)}) %all-gather.17.cloned.1.call-update) | async-done | bytes 1441808 | tf_op jit(solution)/shard_map/all_gather | solution.py:213
  402.4 25.9 %all-gather.21.cloned.1.call-done = bf16[512,1024]{1,0:T(8,128)(2,1)} async-done(((bf16[128,1024]{1,0:T(8,128)(2,1)}), bf16[512,1024]{1,0:T(8,128)(2,1)}) %all-gather.21.cloned.1.call-update) | async-done | bytes 1048592 | tf_op jit(solution)/shard_map/all_gather | solution.py:232
  428.2 26.5 %all-gather.19.cloned.1.call-done = bf16[704,1024]{1,0:T(8,128)(2,1)} async-done(((bf16[704,128]{1,0:T(8,128)(2,1)}), bf16[704,1024]{1,0:T(8,128)(2,1)}) %all-gather.19.cloned.1.call-update) | async-done | bytes 1441808 | tf_op jit(solution)/shard_map/all_gather | solution.py:214
  464.1 43.7 %reduce-scatter.21.cloned.1.call-done = f32[128,1024]{1,0:T(8,128)} async-done(((f32[512,1024]{1,0:T(8,128)}), f32[128,1024]{1,0:T(8,128)}) %reduce-scatter.21.cloned.1.call-update) | async-done | bytes 524304 | tf_op jit(solution)/shard_map/reduce_scatter | solution.py:246
  514.3 24.8 %all-gather.23.cloned.1.call-done = bf16[512,1024]{1,0:T(8,128)(2,1)} async-done(((bf16[128,1024]{1,0:T(8,128)(2,1)}), bf16[512,1024]{1,0:T(8,128)(2,1)}) %all-gather.23.cloned.1.call-update) | async-done | bytes 1048592 | tf_op jit(solution)/shard_map/all_gather | solution.py:255
  546.5 360.5 %while.119 = (s32[]{:T(128)}, f32[1,1,256,128]{3,2,1,0:T(8,128)S(1)}, f32[8,1,1,64,128]{4,3,2,1,0:T(8,128)}, f32[8,1,1,64,128]{4,3,2,1,0:T(8,128)}, f32[8,1,1,64...) while((s32[]{:T(128)}, ...), condition=%wide.region_22.23_spmd.clone, body=%wide.region_13.22_spmd.clone.sunk | while | flops 290205760 | bytes 5457732 | solution.py:109
  954.4 35.7 %reduce-scatter.39.cloned.1.call-done = f32[128,1]{1,0:T(8,128)} async-done(((f32[1024,1]{1,0:T(8,128)}), f32[128,1]{1,0:T(8,128)}) %reduce-scatter.39.cloned.1.call-update) | async-done | bytes 528
  991.5 28.2 %reduce-scatter.23.cloned.1.call-done = bf16[128,1024]{1,0:T(8,128)(2,1)} async-done(((bf16[512,1024]{1,0:T(8,128)(2,1)}), bf16[128,1024]{1,0:T(8,128)(2,1)}) %reduce-scatter.23.cloned.1.call-update) | async-done | bytes 262160 | tf_op jit(solution)/shard_map/reduce_scatter | solution.py:272
  1021.0 40.6 %all-reduce.17 = (f32[1024]{0:T(1024)}, f32[4,2048]{1,0:T(4,128)S(1)}, f32[4]{0:T(128)S(1)}, f32[4]{0:T(128)S(1)}, f32[256]{0:T(256)}, /*index=5*/f32[1024]{0:T(1024)}) all-reduce(f32[1024]{0:T(1024)S(1)} %get-tuple-element.2403, f32[4,2048]{1,0:T(4,128)S(1)} %add_dynamic-update-slice_fusion, ...), channel_id=1, replica_groups=mesh['dp'=8,'tensor'=4] {'dp','tensor'}, use_global_device_ids=true, to_apply=%region_29.30 | all-reduce | flops 10504 | bytes 84032 | tf_op jit(solution)/shard_map/psum | solution.py:309
  1065.6 30.0 %reduce-scatter.33.cloned.1.call-done = f32[128,704]{0,1:T(8,128)} async-done(((f32[1024,704]{0,1:T(8,128)}), f32[128,704]{0,1:T(8,128)}) %reduce-scatter.33.cloned.1.call-update) | async-done | bytes 360464 | tf_op jit(solution)/shard_map/reduce_scatter | solution.py:241
  1095.5 48.6 %reduce-scatter.31.cloned.1.call-done = f32[128,704]{0,1:T(8,128)} async-done(((f32[1024,704]{0,1:T(8,128)}), f32[128,704]{0,1:T(8,128)}) %reduce-scatter.31.cloned.1.call-update) | async-done | bytes 360464 | tf_op jit(solution)/shard_map/reduce_scatter | solution.py:240
  1144.1 48.5 %reduce-scatter.35.cloned.1.call-done = f32[704,128]{1,0:T(8,128)} async-done(((f32[704,1024]{1,0:T(8,128)}), f32[704,128]{1,0:T(8,128)}) %reduce-scatter.35.cloned.1.call-update) | async-done | bytes 360464 | tf_op jit(solution)/shard_map/reduce_scatter | solution.py:242
  1192.6 39.6 %reduce-scatter.29.cloned.1.call-done = f32[256,128]{1,0:T(8,128)} async-done(((f32[256,1024]{1,0:T(8,128)}), f32[256,128]{1,0:T(8,128)}) %reduce-scatter.29.cloned.1.call-update) | async-done | bytes 131088 | tf_op jit(solution)/shard_map/reduce_scatter | solution.py:287
  1232.2 39.7 %reduce-scatter.27.cloned.1.call-done = f32[128,256]{1,0:T(8,128)} async-done(((f32[1024,256]{1,0:T(8,128)}), f32[128,256]{1,0:T(8,128)}) %reduce-scatter.27.cloned.1.call-update) | async-done | bytes 131088 | tf_op jit(solution)/shard_map/reduce_scatter | solution.py:284
  1271.9 44.9 %reduce-scatter.25.cloned.1.call-done = f32[128,512]{1,0:T(8,128)} async-done(((f32[1024,512]{1,0:T(8,128)}), f32[128,512]{1,0:T(8,128)}) %reduce-scatter.25.cloned.1.call-update) | async-done | bytes 262160 | tf_op jit(solution)/shard_map/reduce_scatter | solution.py:283
  (931 shorter events, 661.9 us)
Async XLA Ops:
  7.2 49.6 %all-gather.9.cloned.1.call-start = ((), (), s32[]{:S(2)}) async-start(), calls=%async_computation.12 | async-start | bytes 1310720 | tf_op jit(solution)/shard_map/all_gather | solution.py:183
  10.2 56.7 %all-gather.11.cloned.1.call-start = ((), (), s32[]{:S(2)}) async-start(), calls=%async_computation.13 | async-start | bytes 1179648 | tf_op jit(solution)/shard_map/all_gather | solution.py:177
  10.9 305.2 %reduce-scatter.17.cloned.1.call-start = ((), (), s32[]{:S(2)}) async-start(), calls=%async_computation.14 | async-start | bytes 2621440 | tf_op jit(solution)/shard_map/reduce_scatter | solution.py:203
  77.8 189.6 %copy-start.69 = (f32[256]{0:T(256)S(1)}, f32[256]{0:T(256)}, u32[]{:S(2)}) copy-start(f32[256]{0:T(256)} %param.31) | copy-start | bytes 3076
  272.3 70.0 %all-gather.15.cloned.1.call-start = ((), (), s32[]{:S(2)}) async-start(), calls=%async_computation.16 | async-start | bytes 1622016 | tf_op jit(solution)/shard_map/all_gather | solution.py:212
  272.9 99.4 %all-gather.13.cloned.1.call-start = ((), (), s32[]{:S(2)}) async-start(), calls=%async_computation.15 | async-start | bytes 1310720 | tf_op jit(solution)/shard_map/all_gather | solution.py:216
  317.3 192.3 %copy-start.58 = (f32[128]{0:T(128)}, f32[128]{0:T(128)S(1)}, u32[]{:S(2)}) copy-start(f32[128]{0:T(128)S(1)} %add_rsqrt_fusion.2) | copy-start | bytes 1540
  318.2 80.4 %all-gather.17.cloned.1.call-start = ((), (), s32[]{:S(2)}) async-start(), calls=%async_computation.17 | async-start | bytes 1622016 | tf_op jit(solution)/shard_map/all_gather | solution.py:213
  318.8 109.5 %all-gather.21.cloned.1.call-start = ((), (), s32[]{:S(2)}) async-start(), calls=%async_computation.20 | async-start | bytes 1310720 | tf_op jit(solution)/shard_map/all_gather | solution.py:232
  319.5 135.2 %all-gather.19.cloned.1.call-start = ((), (), s32[]{:S(2)}) async-start(), calls=%async_computation.18 | async-start | bytes 1622016 | tf_op jit(solution)/shard_map/all_gather | solution.py:214
  320.3 187.5 %reduce-scatter.21.cloned.1.call-start = ((), (), s32[]{:S(2)}) async-start(), calls=%async_computation.21 | async-start | bytes 2621440 | tf_op jit(solution)/shard_map/reduce_scatter | solution.py:246
  464.0 75.0 %all-gather.23.cloned.1.call-start = ((), (), s32[]{:S(2)}) async-start(), calls=%async_computation.22 | async-start | bytes 1310720 | tf_op jit(solution)/shard_map/all_gather | solution.py:255
  511.7 441.3 %reduce-scatter.37.cloned.1.call-start = ((), (), s32[]{:S(2)}) async-start(), calls=%async_computation.30 | async-start | bytes 589824
  546.4 362.2 %copy-start.47 = (f32[512]{0:T(512)S(1)}, f32[512]{0:T(512)}, u32[]{:S(2)}) copy-start(f32[512]{0:T(512)} %copy-done.46) | copy-start | bytes 6148
  546.5 362.8 %copy-start.43 = (f32[512]{0:T(512)S(1)}, f32[512]{0:T(512)}, u32[]{:S(2)}) copy-start(f32[512]{0:T(512)} %copy-done.42) | copy-start | bytes 6148
  919.4 70.7 %reduce-scatter.39.cloned.1.call-start = ((), (), s32[]{:S(2)}) async-start(), calls=%async_computation.31 | async-start | bytes 589824
  920.7 99.0 %reduce-scatter.23.cloned.1.call-start = ((), (), s32[]{:S(2)}) async-start(), calls=%async_computation.23 | async-start | bytes 1310720 | tf_op jit(solution)/shard_map/reduce_scatter | solution.py:272
  926.5 136.9 %reduce-scatter.19.cloned.1.call-start = ((), (), s32[]{:S(2)}) async-start(), calls=%async_computation.19 | async-start | bytes 1310720 | tf_op jit(solution)/shard_map/reduce_scatter | solution.py:223
  930.3 165.3 %reduce-scatter.33.cloned.1.call-start = ((), (), s32[]{:S(2)}) async-start(), calls=%async_computation.28 | async-start | bytes 3244032 | tf_op jit(solution)/shard_map/reduce_scatter | solution.py:241
  934.0 210.1 %reduce-scatter.31.cloned.1.call-start = ((), (), s32[]{:S(2)}) async-start(), calls=%async_computation.27 | async-start | bytes 3244032 | tf_op jit(solution)/shard_map/reduce_scatter | solution.py:240
  937.9 254.7 %reduce-scatter.35.cloned.1.call-start = ((), (), s32[]{:S(2)}) async-start(), calls=%async_computation.29 | async-start | bytes 3244032 | tf_op jit(solution)/shard_map/reduce_scatter | solution.py:242
  942.8 289.4 %reduce-scatter.29.cloned.1.call-start = ((), (), s32[]{:S(2)}) async-start(), calls=%async_computation.26 | async-start | bytes 1179648 | tf_op jit(solution)/shard_map/reduce_scatter | solution.py:287
  945.6 326.3 %reduce-scatter.27.cloned.1.call-start = ((), (), s32[]{:S(2)}) async-start(), calls=%async_computation.25 | async-start | bytes 1179648 | tf_op jit(solution)/shard_map/reduce_scatter | solution.py:284
  948.1 368.7 %reduce-scatter.25.cloned.1.call-start = ((), (), s32[]{:S(2)}) async-start(), calls=%async_computation.24 | async-start | bytes 2359296 | tf_op jit(solution)/shard_map/reduce_scatter | solution.py:283
  (71 other events, 1352.1 us)
Sparse Core Ops, SparseCore 0:
  10.3 30.6 all-gather.8
  42.9 23.8 all-gather.10
  272.5 43.6 reduce-scatter.16
  317.9 24.3 all-gather.14
  344.3 27.9 all-gather.12
  374.0 24.5 all-gather.16
  400.2 27.9 all-gather.20
  430.1 24.5 all-gather.18
  464.1 43.6 reduce-scatter.20
  511.8 27.1 all-gather.22
  919.5 33.4 reduce-scatter.36
  955.9 34.1 reduce-scatter.38
  992.4 27.2 reduce-scatter.22
  1021.9 26.4 reduce-scatter.18
  1052.2 43.2 reduce-scatter.32
  1099.3 44.6 reduce-scatter.30
  1147.9 44.6 reduce-scatter.34
  1196.2 35.9 reduce-scatter.28
  1236.0 35.9 reduce-scatter.26
  1275.6 41.1 reduce-scatter.24
where the time goes:
time: 1340 us; the launch traced here: 1320 us
  waiting for transfers between devices  564 us (42%)
  matrix products  467 us (35%)
  other arithmetic  109 us (8%)
  blocking collectives  81.7 us (6%)
  local copies, waits for them, and re-layouts  80.6 us (6%)
  between operations  17.5 us (1%)
    dot_general x408, matrix products, contract(): return jnp.einsum(form, left, right, precision=HIGHEST)  413 us
    dot_general x22, matrix products, matmul(): return jnp.dot(left, right, preferred_element_type=jnp.float32)  54.4 us
    reduce_scatter x1, waiting for transfers between devices, local(): lax.psum_scatter(grad_fgate, 'dp', scatter_dimension=0, tiled=True)  48.6 us
    reduce_scatter x1, waiting for transfers between devices, local(): lax.psum_scatter(grad_down, 'dp', scatter_dimension=1, tiled=True)  48.5 us
    dynamic_update_slice x40, other arithmetic, delta_blocks(): lax.scan(advance, initial, (to_blocks(query), to_blocks(keys), to_blocks(...  46.8 us
    reduce_scatter x1, waiting for transfers between devices, local(): lax.psum_scatter(grad_qkv, 'dp', scatter_dimension=0, tiled=True)  44.9 us
    reduce_scatter x1, waiting for transfers between devices, local(): lax.psum_scatter(matmul(gate_rows, full_fgate.T) + matmul(up_rows, full_f...  43.7 us
    reduce_scatter x1, waiting for transfers between devices, local(): lax.psum_scatter(matmul(lax.slice_in_dim(mixed, 0, lax.axis_size('tensor'...  43.2 us
  transfers between devices with their start and end apart: 20, of which 18 were waited for; matrix products, arithmetic and copies ran while one was open for 4% of the time, Pallas kernels for 0%

commit v1 on v0

v1 whole, which is shorter than its diff:
```python
import jax
import jax.numpy as jnp
from jax import lax
from jax.experimental import pallas as pl
from jax.sharding import PartitionSpec as P

DK = 128
DV = 256
STRETCH = 128
LEN = 512


HIGHEST = lax.Precision.HIGHEST


def matmul(left, right):
    return jnp.dot(left, right, preferred_element_type=jnp.float32)


def short_conv(mixer_in, conv_weight, segment):
    taps = conv_weight.shape[0]
    total = conv_weight[taps - 1] * mixer_in
    for offset in range(1, taps):
        shifted = jnp.concatenate(
            [jnp.zeros((offset, mixer_in.shape[1]), mixer_in.dtype), mixer_in[:-offset]], 0
        )
        earlier = jnp.concatenate([jnp.full((offset,), -1, jnp.int32), segment[:-offset]], 0)
        same_doc = (earlier == segment).astype(mixer_in.dtype)
        total = total + conv_weight[taps - 1 - offset] * shifted * same_doc[:, None]
    return jax.nn.silu(total)


def split_heads(activated, heads):
    grouped = activated.reshape(activated.shape[0], heads, 2 * DK + DV)
    query = grouped[..., :DK]
    keys = grouped[..., DK : 2 * DK]
    values = grouped[..., 2 * DK :]
    query = query * lax.rsqrt(jnp.sum(query * query, -1, keepdims=True) + 1e-06) * DK ** (-0.5)
    keys = keys * lax.rsqrt(jnp.sum(keys * keys, -1, keepdims=True) + 1e-06)
    return (query, keys, values)


def gated_norm(output_heads, gate_in, out_gain):
    rows, heads = (output_heads.shape[0], output_heads.shape[1])
    gate_heads = gate_in.reshape(rows, heads, DV)
    normed = (
        output_heads
        * lax.rsqrt(jnp.mean(output_heads * output_heads, -1, keepdims=True) + 1e-05)
        * out_gain
    )
    return (normed * jax.nn.silu(gate_heads)).reshape(rows, heads * DV)


def dot(left, right, left_dim, right_dim):
    return lax.dot_general(
        left,
        right,
        (((left_dim,), (right_dim,)), ((), ())),
        precision=HIGHEST,
        preferred_element_type=jnp.float32,
    )


def strictly_below():
    row = lax.broadcasted_iota(jnp.int32, (STRETCH, STRETCH), 0)
    column = lax.broadcasted_iota(jnp.int32, (STRETCH, STRETCH), 1)
    return row, column


def unit_lower_inverses(lowers):
    row, column = strictly_below()
    span = 1
    results = None
    while span < STRETCH:
        pair = (row // (2 * span) == column // (2 * span)) & (row // span != column // span)
        corners = [jnp.where(pair, lower, 0.0) for lower in lowers]
        if results is None:
            identity = (row == column).astype(jnp.float32)
            results = [identity - corner for corner in corners]
        else:
            halves = [dot(corner, result, 1, 0) for corner, result in zip(corners, results)]
            results = [result - dot(result, half, 1, 0) for result, half in zip(results, halves)]
        span = span * 2
    return results


def forward_kernel(q, k, v, strength, carry, tail, ratio, last, o, u, states, inverses):
    blocks = q.shape[0] // STRETCH
    row, column = strictly_below()
    lowers = []
    for i in range(blocks):
        here = pl.ds(i * STRETCH, STRETCH)
        kk = dot(k[here, :], k[here, :], 1, 1)
        lowers.append(jnp.where(row > column, strength[here, :] * ratio[here, :] * kk, 0.0))
    inverse_list = unit_lower_inverses(lowers)
    state = jnp.zeros((v.shape[1], k.shape[1]), jnp.float32)
    for i in range(blocks):
        here = pl.ds(i * STRETCH, STRETCH)
        states[pl.ds(i * v.shape[1], v.shape[1]), :] = state
        inverses[here, :] = inverse_list[i]
        keys, query, carried = k[here, :], q[here, :], carry[here, :]
        target = strength[here, :] * (v[here, :] - carried * dot(keys, state, 1, 1))
        update = dot(inverse_list[i], target, 1, 0)
        u[here, :] = update
        weights = ratio[here, :] * dot(query, keys, 1, 1)
        o[here, :] = carried * dot(query, state, 1, 1) + dot(weights, update, 1, 0)
        state = last[pl.ds(i, 1), :] * state + dot(update * tail[here, :], keys, 0, 0)


def backward_kernel(
    q, k, v, strength, carry, tail, ratio, last, u, states, inverses, do,
    dq, dk, dv, dstrength, dcarry, dtail, dratio, dlast,
):
    blocks = q.shape[0] // STRETCH
    row, column = strictly_below()
    dstate = jnp.zeros((v.shape[1], k.shape[1]), jnp.float32)
    for i in reversed(range(blocks)):
        here = pl.ds(i * STRETCH, STRETCH)
        state = states[pl.ds(i * v.shape[1], v.shape[1]), :]
        keys, query, carried, beta = k[here, :], q[here, :], carry[here, :], strength[here, :]
        ends, scale, update, grad = tail[here, :], ratio[here, :], u[here, :], do[here, :]
        kk = dot(keys, keys, 1, 1)
        qk = dot(query, keys, 1, 1)
        key_state = dot(keys, state, 1, 1)
        query_state = dot(query, state, 1, 1)
        rest = v[here, :] - carried * key_state
        key_dstate = dot(keys, dstate, 1, 1)
        dupdate = dot(scale * qk, grad, 0, 0) + ends * key_dstate
        dtail[here, :] = jnp.sum(key_dstate * update, -1, keepdims=True)
        dweights = dot(grad, update, 1, 1)
        dqk = dweights * scale
        dtarget = dot(inverses[here, :], dupdate, 0, 0)
        dlower = jnp.where(row > column, -dot(dtarget, update, 1, 1), 0.0)
        dstrength[here, :] = jnp.sum(dtarget * rest, -1, keepdims=True) + jnp.sum(
            dlower * scale * kk, -1, keepdims=True
        )
        drest = beta * dtarget
        dv[here, :] = drest
        dcarry[here, :] = jnp.sum(grad * query_state - drest * key_state, -1, keepdims=True)
        dratio[here, :] = dweights * qk + dlower * beta * kk
        dkk = dlower * beta * scale
        dquery_state = carried * grad
        dkey_state = -carried * drest
        dq[here, :] = dot(dquery_state, state, 1, 0) + dot(dqk, keys, 1, 0)
        dk[here, :] = (
            dot(update * ends, dstate, 1, 0)
            + dot(dqk, query, 0, 0)
            + dot(dkey_state, state, 1, 0)
            + dot(dkk, keys, 1, 0)
            + dot(dkk, keys, 0, 0)
        )
        dlast[pl.ds(i, 1), :] = jnp.sum(dstate * state, 0, keepdims=True)
        dstate = (
            last[pl.ds(i, 1), :] * dstate
            + dot(dquery_state, query, 0, 0)
            + dot(dkey_state, keys, 0, 0)
        )


def shaped(*shapes):
    return tuple(jax.ShapeDtypeStruct(shape, jnp.float32) for shape in shapes)


def run_kernel(kernel, out_shape, arrays):
    rows = arrays[0].shape[0]
    return pl.pallas_call(
        kernel,
        out_shape=out_shape,
        cost_estimate=pl.CostEstimate(
            flops=rows * 80_000_000, transcendentals=0, bytes_accessed=rows * 16384
        ),
    )(*arrays)


def delta_run(arrays):
    q, k, v = arrays[:3]
    rows, wide = v.shape
    blocks = rows // STRETCH
    return run_kernel(
        forward_kernel,
        shaped((rows, wide), (rows, wide), (blocks * wide, k.shape[1]), (rows, STRETCH)),
        arrays,
    )


@jax.custom_vjp
def delta_core(*arrays):
    return delta_run(arrays)[0]


def delta_core_forward(*arrays):
    o, u, states, inverses = delta_run(arrays)
    return o, (arrays, u, states, inverses)


def delta_core_backward(saved, do):
    arrays, u, states, inverses = saved
    return tuple(
        run_kernel(
            backward_kernel,
            shaped(*[array.shape for array in arrays]),
            arrays + (u, states, inverses, do),
        )
    )


delta_core.defvjp(delta_core_forward, delta_core_backward)


def delta_blocks(query, keys, values, strength, log_decay, segment):
    rows, heads = (query.shape[0], query.shape[1])
    blocks = rows // STRETCH
    seg = segment.reshape(blocks, STRETCH)
    before = jnp.concatenate([jnp.full((1,), -1, jnp.int32), seg[:-1, -1]], 0)
    position = jnp.arange(STRETCH)
    inclusive = position[:, None] >= position[None, :]
    keep = (seg[:, :, None] == seg[:, None, :]) & inclusive
    at_start = (seg == before[:, None]).astype(jnp.float32)
    outs = []
    for head in range(heads):
        decay = log_decay[:, head].reshape(blocks, STRETCH)
        cumulative = jnp.sum(jnp.where(inclusive, decay[:, None, :], 0.0), -1)
        ratio = jnp.exp(
            jnp.where(keep, cumulative[:, :, None] - cumulative[:, None, :], 0.0)
        ) * keep.astype(jnp.float32)
        carry = jnp.exp(cumulative) * at_start
        outs.append(
            delta_core(
                query[:, head],
                keys[:, head],
                values[:, head],
                strength[:, head][:, None],
                carry.reshape(rows, 1),
                ratio[:, -1, :].reshape(rows, 1),
                ratio.reshape(rows, STRETCH),
                jnp.broadcast_to(carry[:, -1:], (blocks, query.shape[-1])),
            )
        )
    return jnp.stack(outs, 1)


def mixer_core(
    segment, mixer_in, gate_in, beta_in, decay_in, conv_weight, a_log, dt_bias, out_gain
):
    heads = a_log.shape[0]
    query, keys, values = split_heads(short_conv(mixer_in, conv_weight, segment), heads)
    strength = jax.nn.sigmoid(beta_in)
    log_decay = -jnp.exp(a_log) * jax.nn.softplus(decay_in + dt_bias)
    output_heads = delta_blocks(query, keys, values, strength, log_decay, segment)
    return gated_norm(output_heads, gate_in, out_gain)


def root_mean_square_forward(rows):
    inverse_scale = lax.rsqrt(jnp.mean(rows * rows, -1, keepdims=True) + 1e-06)
    return (rows * inverse_scale, inverse_scale)


def root_mean_square_backward(normalized_input, inverse_scale, norm_gain, upstream_gradient):
    scaled_rows = upstream_gradient * norm_gain
    return (
        inverse_scale
        * (
            scaled_rows
            - normalized_input * jnp.mean(scaled_rows * normalized_input, -1, keepdims=True)
        ),
        jnp.sum(upstream_gradient * normalized_input, 0),
    )


def matmul_t(left, right):
    return lax.dot_general(
        left, right, (((1,), (1,)), ((), ())), preferred_element_type=jnp.float32
    )


def scatter_sum(partial_sums, axis):
    count = lax.axis_size(axis)
    rows, columns = partial_sums.shape
    pieces = partial_sums.astype(jnp.bfloat16).reshape(count, rows // count, columns)
    received = lax.all_to_all(pieces, axis, 0, 0)
    return jnp.sum(received.astype(jnp.float32), 0)


def local(
    block_input,
    segment_ids,
    attention_norm_gain,
    w_qkv,
    w_og,
    w_beta,
    w_alpha,
    conv_weight,
    a_log,
    dt_bias,
    out_gain,
    w_out,
    ffn_gain,
    w_ffn_gate,
    w_ffn_up,
    w_ffn_down,
    cotangent,
):
    tensor_count = lax.axis_size("tensor")
    local_rows = block_input.shape[0]
    wide_qkv, wide_og, heads_here = w_qkv.shape[1], w_og.shape[1], w_beta.shape[1]
    wide_in = wide_qkv + wide_og + 2 * heads_here
    hidden_here = w_ffn_gate.shape[1]
    residual_input = block_input.astype(jnp.float32)
    attention_normalized_input, attention_scale = root_mean_square_forward(residual_input)
    local_normed_rows = (attention_normalized_input * attention_norm_gain).astype(jnp.bfloat16)
    attention_normed = lax.all_gather(local_normed_rows, "tensor", axis=0, tiled=True)
    full_mixer = lax.all_gather(
        jnp.concatenate([w_qkv, w_og, w_beta, w_alpha, w_out.T], 1), "dp", axis=0, tiled=True
    )
    full_in, full_out_t = full_mixer[:, :wide_in], full_mixer[:, wide_in:]
    full_ffn = lax.all_gather(
        jnp.concatenate([w_ffn_gate, w_ffn_up, w_ffn_down.T], 1), "dp", axis=0, tiled=True
    )
    full_gate_up, full_down_t = full_ffn[:, : 2 * hidden_here], full_ffn[:, 2 * hidden_here :]
    grad_all = lax.all_gather(cotangent, "tensor", axis=0, tiled=True)
    rows_all = attention_normed.shape[0]
    seq_count = rows_all // LEN
    projected = matmul(attention_normed, full_in).reshape(seq_count, LEN, -1)
    cuts = (wide_qkv, wide_qkv + wide_og, wide_qkv + wide_og + heads_here)

    def core_all(projected, conv_weight, a_log, dt_bias, out_gain):
        mixer_in, gate_in, beta_in, decay_in = jnp.split(projected, cuts, axis=-1)
        return jnp.stack(
            [
                mixer_core(
                    segment_ids[i], mixer_in[i], gate_in[i], beta_in[i], decay_in[i],
                    conv_weight, a_log, dt_bias, out_gain,
                )
                for i in range(seq_count)
            ]
        )

    mixed_full, core_back = jax.vjp(core_all, projected, conv_weight, a_log, dt_bias, out_gain)
    mixed = mixed_full.reshape(rows_all, -1).astype(jnp.bfloat16)
    resid_mid = residual_input + scatter_sum(matmul_t(mixed, full_out_t), "tensor")
    hhat, scale_ffn = root_mean_square_forward(resid_mid)
    normed_ffn_local = (hhat * ffn_gain).astype(jnp.bfloat16)
    normed_ffn = lax.all_gather(normed_ffn_local, "tensor", axis=0, tiled=True)
    gate_up = matmul(normed_ffn, full_gate_up)
    fgate, fup = gate_up[:, :hidden_here], gate_up[:, hidden_here:]
    dhidden = matmul(grad_all, full_down_t)
    sigma = jax.nn.sigmoid(fgate)
    hidden = (fgate * sigma * fup).astype(jnp.bfloat16)
    dfgate = (dhidden * fup * sigma * (1.0 + fgate * (1.0 - sigma))).astype(jnp.bfloat16)
    dfup = (dhidden * fgate * sigma).astype(jnp.bfloat16)
    dgate_up = jnp.concatenate([dfgate, dfup], 1)
    dnormed_ffn = scatter_sum(matmul_t(dgate_up, full_gate_up), "tensor")
    block_output = (
        resid_mid + scatter_sum(matmul_t(hidden, full_down_t), "tensor")
    ).astype(jnp.bfloat16)
    ffn_summed = scatter_sum(
        jnp.concatenate(
            [matmul(normed_ffn.T, dfgate), matmul(normed_ffn.T, dfup), matmul(grad_all.T, hidden)], 1
        ),
        "dp",
    )
    dresid_norm, grad_ffn_gain = root_mean_square_backward(hhat, scale_ffn, ffn_gain, dnormed_ffn)
    dresid = cotangent.astype(jnp.float32) + dresid_norm
    dresid_b = dresid.astype(jnp.bfloat16)
    dresid_all = lax.all_gather(dresid_b, "tensor", axis=0, tiled=True)
    dmixed = matmul(dresid_all, full_out_t).reshape(seq_count, LEN, -1)
    dprojected, grad_conv, grad_alog, grad_dt, grad_ogain = core_back(dmixed)
    dprojected_b = dprojected.reshape(rows_all, -1).astype(jnp.bfloat16)
    attention_normed_gradient = scatter_sum(matmul_t(dprojected_b, full_in), "tensor")
    mixer_summed = scatter_sum(
        jnp.concatenate(
            [matmul(attention_normed.T, dprojected_b), matmul(dresid_all.T, mixed)], 1
        ),
        "dp",
    )
    norm_input_gradient, attention_gain_gradient = root_mean_square_backward(
        attention_normalized_input, attention_scale, attention_norm_gain, attention_normed_gradient
    )
    input_grad = dresid + norm_input_gradient
    everywhere = [attention_gain_gradient, grad_ffn_gain, grad_ogain]
    here = [grad_conv.reshape(-1), grad_alog, grad_dt]
    lengths = [item.shape[0] for item in everywhere + here]
    ends = [sum(lengths[: i + 1]) for i in range(len(lengths))]
    packed = jnp.concatenate(everywhere + here)
    packed = jnp.pad(packed, (0, -packed.shape[0] % 1024)).reshape(8, -1)
    gathered = lax.all_gather(packed, ("dp", "tensor"), axis=0, tiled=True)
    gathered = gathered.reshape(-1, tensor_count, packed.size)
    by_place = jnp.sum(gathered, 0)
    attn_gain_grad, ffn_gain_grad, out_gain_grad = jnp.split(
        jnp.sum(by_place[:, : ends[2]], 0), ends[:2]
    )
    own = lax.dynamic_index_in_dim(by_place, lax.axis_index("tensor"), 0, keepdims=False)
    conv_weight_grad = own[ends[2] : ends[3]].reshape(conv_weight.shape)
    a_log_grad = own[ends[3] : ends[4]]
    dt_bias_grad = own[ends[4] : ends[5]]
    return (
        block_output,
        input_grad,
        attn_gain_grad,
        mixer_summed[:, : cuts[0]],
        mixer_summed[:, cuts[0] : cuts[1]],
        mixer_summed[:, cuts[1] : cuts[2]],
        mixer_summed[:, cuts[2] : wide_in],
        conv_weight_grad,
        a_log_grad,
        dt_bias_grad,
        out_gain_grad,
        mixer_summed[:, wide_in:].T,
        ffn_gain_grad,
        ffn_summed[:, :hidden_here],
        ffn_summed[:, hidden_here : 2 * hidden_here],
        ffn_summed[:, 2 * hidden_here :].T,
    )


def solution(mesh):
    placed = (
        P(("dp", "tensor"), None),
        P("dp", None),
        P(),
        P("dp", "tensor"),
        P("dp", "tensor"),
        P("dp", "tensor"),
        P("dp", "tensor"),
        P(None, "tensor"),
        P("tensor"),
        P("tensor"),
        P(),
        P("tensor", "dp"),
        P(),
        P("dp", "tensor"),
        P("dp", "tensor"),
        P("tensor", "dp"),
        P(("dp", "tensor"), None),
    )
    return jax.shard_map(
        local,
        mesh=mesh,
        in_specs=placed,
        out_specs=(
            P(("dp", "tensor"), None),
            P(("dp", "tensor"), None),
            P(),
            P("dp", "tensor"),
            P("dp", "tensor"),
            P("dp", "tensor"),
            P("dp", "tensor"),
            P(None, "tensor"),
            P("tensor"),
            P("tensor"),
            P(),
            P("tensor", "dp"),
            P(),
            P("dp", "tensor"),
            P("dp", "tensor"),
            P("tensor", "dp"),
        ),
        check_vma=False,
    )
```

time: 1340 us -> 525 us (0.39)
  matrix products: 467 us -> 39 us
  waiting for transfers between devices: 564 us -> 223 us
  other arithmetic: 109 us -> 50.9 us
  local copies, waits for them, and re-layouts: 80.6 us -> 33 us
  blocking collectives: 81.7 us -> 108 us
  Pallas kernels: 0 us -> 21 us
  starting transfers between devices: 1.22 us -> 22 us
    dot_general x408 -> x4, matrix products: 413 us -> 10.8 us  [matmul_t(): lax.dot_general(left, right, (((1,), (1,)), ((), ())), preferred_element_...]
    reduce_scatter x10 -> x0, waiting for transfers between devices: 366 us -> none  [the longest x1 48.6 us: local(): lax.psum_scatter(grad_fgate, 'dp', scatter_dimension=0, tiled=True)]
    all_to_all x0 -> x5, waiting for transfers between devices: none -> 49 us  [scatter_sum(): received = lax.all_to_all(pieces, axis, 0, 0)]
    dynamic_update_slice x42 -> x0, other arithmetic: 46.9 us -> none  [the longest x40 46.8 us: delta_blocks(): lax.scan(advance, initial, (to_blocks(query), to_blocks(keys), to_blocks(...]
    psum x1 -> x0, blocking collectives: 40.6 us -> none  [local(): lax.psum((attention_gain_gradient, grad_ffn_gain, grad_ogain, conv_full,...]
    unnamed x22 -> x6, waiting for transfers between devices: 40.1 us -> 0.61 us
    all_gather x4 -> x1, blocking collectives: 41 us -> 77.6 us  [local(): gathered = lax.all_gather(packed, ('dp', 'tensor'), axis=0, tiled=True)]
    all_to_all x0 -> x1, blocking collectives: none -> 30.8 us  [scatter_sum(): received = lax.all_to_all(pieces, axis, 0, 0)]
  transfers between devices with their start and end apart: 20 -> 11, of which waited for: 18 -> 9; matrix products, arithmetic and copies ran while one was open for 4% -> 14% of each run, Pallas kernels for 0% -> 2%
where the time goes in v1:
time: 525 us; the launch traced here: 515 us
  waiting for transfers between devices  223 us (42%)
  blocking collectives  108 us (21%)
  other arithmetic  50.9 us (10%)
  matrix products  39 us (7%)
  local copies, waits for them, and re-layouts  33 us (6%)
  starting transfers between devices  22 us (4%)
  Pallas kernels  21 us (4%)
  between operations  17.5 us (3%)
    all_gather x1, blocking collectives, local(): gathered = lax.all_gather(packed, ('dp', 'tensor'), axis=0, tiled=True)  77.6 us
    all_to_all x5, waiting for transfers between devices, scatter_sum(): received = lax.all_to_all(pieces, axis, 0, 0)  49 us
    all_gather x1, waiting for transfers between devices, local(): lax.all_gather(jnp.concatenate([w_ffn_gate, w_ffn_up, w_ffn_down.T], 1),...  39.1 us
    all_gather x1, waiting for transfers between devices, local(): dresid_all = lax.all_gather(dresid_b, 'tensor', axis=0, tiled=True)  32.2 us
    all_gather x1, waiting for transfers between devices, local(): lax.all_gather(jnp.concatenate([w_qkv, w_og, w_beta, w_alpha, w_out.T], 1...  30.9 us
    all_to_all x1, blocking collectives, scatter_sum(): received = lax.all_to_all(pieces, axis, 0, 0)  30.8 us
    dot_general x9, matrix products, matmul(): return jnp.dot(left, right, preferred_element_type=jnp.float32)  28.2 us
    all_gather x1, waiting for transfers between devices, local(): grad_all = lax.all_gather(cotangent, 'tensor', axis=0, tiled=True)  23.9 us
  transfers between devices with their start and end apart: 11, of which 9 were waited for; matrix products, arithmetic and copies ran while one was open for 14% of the time, Pallas kernels for 2%

profile of v1, /device:TPU:0, one launch (start us, length us, event | category | flops | bytes accessed | tf_op | source)
XLA Modules:
  0.0 514.5 jit_solution(3577274525528385141)
XLA Ops:
  17.5 23.5 %all-gather.7.cloned.1.call-done = bf16[512,1024]{1,0:T(8,128)(2,1)} async-done(((bf16[128,1024]{1,0:T(8,128)(2,1)}), bf16[512,1024]{1,0:T(8,128)(2,1)}) %all-gather.7.cloned.1.call-update) | async-done | bytes 1048592 | tf_op jit(solution)/shard_map/all_gather | solution.py:311
  40.9 30.9 %all-gather.9.cloned.1.call-done = bf16[1024,1026]{1,0:T(8,128)(2,1)} async-done(((bf16[128,1026]{1,0:T(8,128)(2,1)}), bf16[1024,1026]{1,0:T(8,128)(2,1)}) %all-gather.9.cloned.1.call-update) | async-done | bytes 2101264 | tf_op jit(solution)/shard_map/all_gather | solution.py:312
  71.8 3.1 fusion.13
  91.8 9.7 %jvp__.1 = (f32[512,256]{1,0:T(8,128)}, f32[512,256]{1,0:T(8,128)}, f32[1024,128]{1,0:T(8,128)}, f32[512,128]{1,0:T(8,128)}) custom-call(f32[512,128]{1,0:T(8,128)} %get-tuple-element.214.q, f32[512,128]{1,0:T(8,128)} %get-tuple-element.213.k, f32[512,256]{1,0:T(8,128)} %slice_bitcast_fusion.5.v, f32[512,1]{1,0:T(8,128)} %get-tuple-element.203.strength, ...), custom_call_target="tpu_custom_call" | custom-call | flops 40960000000 | bytes 8388608 | tf_op jit(solution)/shard_map/jvp()/pallas_call | solution.py:166
  106.4 30.8 %all_to_all.30 = bf16[4,128,1024]{2,1,0:T(8,128)(2,1)S(1)} all-to-all(bf16[4,128,1024]{2,1,0:T(8,128)(2,1)S(1)} %bitcast.208), channel_id=1, replica_groups=mesh['dp'=8,'tensor'=4] {'tensor'}, dimensions={0} | all-to-all | bytes 2097152 | tf_op jit(solution)/shard_map/all_to_all | solution.py:280
  141.6 23.7 %all-gather.11.cloned.1.call-done = bf16[512,1024]{1,0:T(8,128)(2,1)} async-done(((bf16[128,1024]{1,0:T(8,128)(2,1)}), bf16[512,1024]{1,0:T(8,128)(2,1)}) %all-gather.11.cloned.1.call-update) | async-done | bytes 1048592 | tf_op jit(solution)/shard_map/all_gather | solution.py:343
  165.2 39.1 %all-gather.13.cloned.1.call-done = bf16[1024,2112]{0,1:T(8,128)(2,1)} async-done(((bf16[128,2112]{0,1:T(8,128)(2,1)}), bf16[1024,2112]{0,1:T(8,128)(2,1)}) %all-gather.13.cloned.1.call-update) | async-done | bytes 4325392 | tf_op jit(solution)/shard_map/all_gather | solution.py:316
  204.3 5.5 %fusion.2 = f32[512,1408]{1,0:T(8,128)} fusion(bf16[512,1024]{1,0:T(8,128)(2,1)} %all-gather.11.cloned.1.call-done, bf16[1024,2112]{0,1:T(8,128)(2,1)} %all-gather.13.cloned.1.call-done), kind=kOutput, calls=%fused_computation.5 | convolution fusion | flops 1476395008 | bytes 6815744 | tf_op jit(solution)/shard_map/dot_general | solution.py:17
  209.8 23.9 %all-gather.15.cloned.1.call-done = bf16[512,1024]{1,0:T(8,128)(2,1)} async-done(((bf16[128,1024]{1,0:T(8,128)(2,1)}), bf16[512,1024]{1,0:T(8,128)(2,1)}) %all-gather.15.cloned.1.call-update) | async-done | bytes 1048592 | tf_op jit(solution)/shard_map/all_gather | solution.py:320
  233.7 5.1 fusion.10
  241.6 4.2 all-to-all-start.2
  249.7 21.8 %all-to-all-done.2 = bf16[4,128,1024]{2,1,0:T(8,128)(2,1)} async-done(((bf16[4,128,1024]{2,1,0:T(8,128)(2,1)}), bf16[4,128,1024]{2,1,0:T(8,128)(2,1)}, u32[]{:S(2)}, u32[]{:S(2)}) %all-to-all-start.2) | async-done | bytes 1048608 | tf_op jit(solution)/shard_map/all_to_all | solution.py:280
  276.0 3.6 convolution_convert_fusion.4
  279.6 4.2 all-to-all-start.1
  291.0 32.2 %all-gather.17.cloned.1.call-done = bf16[512,1024]{1,0:T(8,128)(2,1)} async-done(((bf16[128,1024]{1,0:T(8,128)(2,1)}), bf16[512,1024]{1,0:T(8,128)(2,1)}) %all-gather.17.cloned.1.call-update) | async-done | bytes 1048592 | tf_op jit(solution)/shard_map/all_gather | solution.py:365
  323.2 3.7 multiply_reduce_fusion.4
  327.9 4.8 all-to-all-start.5
  332.7 11.2 %transpose_jvp___.1 = (f32[512,128]{1,0:T(8,128)}, f32[512,128]{1,0:T(8,128)}, f32[512,256]{1,0:T(8,128)}, f32[512,1]{1,0:T(8,128)}, f32[512,1]{1,0:T(8,128)}, /...) custom-call(f32[512,128]{1,0:T(8,128)} %get-tuple-element.214.q, f32[512,128]{1,0:T(8,128)} %get-tuple-element.213.k, ...), custom_call_target="tpu_custom_call" | custom-call | flops 40960000000 | bytes 8388608 | tf_op jit(solution)/shard_map/transpose(jvp())/pallas_call | solution.py:228
  367.3 15.7 %all-to-all-done.5 = bf16[8,128,2112]{1,2,0:T(8,128)(2,1)} async-done(((bf16[8,128,2112]{1,2,0:T(8,128)(2,1)}), bf16[8,128,2112]{1,2,0:T(8,128)(2,1)}, u32[]{:S(2)}, u32[]{:S(2)}) %all-to-all-start.5) | async-done | bytes 4325408 | tf_op jit(solution)/shard_map/all_to_all | solution.py:280
  383.0 3.5 all-to-all-start.3
  398.0 11.6 %all-to-all-done.3 = bf16[4,128,1024]{2,1,0:T(8,128)(2,1)S(1)} async-done(((bf16[4,128,1024]{2,1,0:T(8,128)(2,1)}), bf16[4,128,1024]{2,1,0:T(8,128)(2,1)S(1)}, u32[]{:S(2)}, u32[]{:S(2)}) %all-to-all-start.3) | async-done | bytes 1048608 | tf_op jit(solution)/shard_map/all_to_all | solution.py:280
  409.6 4.9 all-to-all-start.4
  414.5 2.9 convert_reduce_fusion
  419.8 77.6 %all_gather.27 = f32[256,640]{1,0:T(8,128)} all-gather(f32[8,640]{1,0:T(8,128)S(1)} %reshape.528), channel_id=1, replica_groups=mesh['dp'=8,'tensor'=4] {'dp','tensor'}, dimensions={0}, use_global_device_ids=true | all-gather | bytes 675840 | tf_op jit(solution)/shard_map/all_gather | solution.py:386
  (272 shorter events, 99.9 us)
Async XLA Ops:
  7.2 33.7 %all-gather.7.cloned.1.call-start = ((), (), s32[]{:S(2)}) async-start(), calls=%async_computation.6 | async-start | bytes 1310720 | tf_op jit(solution)/shard_map/all_gather | solution.py:311
  8.3 66.5 %copy-start.59 = (f32[128]{0:T(128)}, f32[128]{0:T(128)S(1)}, u32[]{:S(2)}) copy-start(f32[128]{0:T(128)S(1)} %add_rsqrt_fusion.3) | copy-start | bytes 1540
  10.2 61.6 %all-gather.9.cloned.1.call-start = ((), (), s32[]{:S(2)}) async-start(), calls=%async_computation.7 | async-start | bytes 2654208 | tf_op jit(solution)/shard_map/all_gather | solution.py:312
  14.5 150.7 %all-gather.11.cloned.1.call-start = ((), (), s32[]{:S(2)}) async-start(), calls=%async_computation.8 | async-start | bytes 1310720 | tf_op jit(solution)/shard_map/all_gather | solution.py:343
  17.4 57.9 %copy-start.36 = (f32[512]{0:T(512)}, f32[512]{0:T(512)S(1)}, u32[]{:S(2)}) copy-start(f32[512]{0:T(512)S(1)} %get-tuple-element.232) | copy-start | bytes 6148
  17.4 57.9 %copy-start.38 = (f32[512]{0:T(512)}, f32[512]{0:T(512)S(1)}, u32[]{:S(2)}) copy-start(f32[512]{0:T(512)S(1)} %get-tuple-element.234) | copy-start | bytes 6148
  17.4 57.9 %copy-start.46 = (f32[512]{0:T(512)}, f32[512]{0:T(512)S(1)}, u32[]{:S(2)}) copy-start(f32[512]{0:T(512)S(1)} %get-tuple-element.233) | copy-start | bytes 6148
  17.4 57.9 %copy-start.34 = (f32[1,512]{1,0:T(1,128)}, f32[1,512]{1,0:T(1,128)S(1)}, u32[]{:S(2)}) copy-start(f32[1,512]{1,0:T(1,128)S(1)} %get-tuple-element.225) | copy-start | bytes 6148
  17.4 57.9 %copy-start.40 = (f32[1,512]{1,0:T(1,128)}, f32[1,512]{1,0:T(1,128)S(1)}, u32[]{:S(2)}) copy-start(f32[1,512]{1,0:T(1,128)S(1)} %get-tuple-element.227) | copy-start | bytes 6148
  17.4 57.9 %copy-start.42 = (f32[1,512]{1,0:T(1,128)}, f32[1,512]{1,0:T(1,128)S(1)}, u32[]{:S(2)}) copy-start(f32[1,512]{1,0:T(1,128)S(1)} %get-tuple-element.226) | copy-start | bytes 6148
  17.5 57.9 %copy-start.44 = (f32[1,512]{1,0:T(1,128)}, f32[1,512]{1,0:T(1,128)S(1)}, u32[]{:S(2)}) copy-start(f32[1,512]{1,0:T(1,128)S(1)} %get-tuple-element.228) | copy-start | bytes 6148
  139.0 65.3 %all-gather.13.cloned.1.call-start = ((), (), s32[]{:S(2)}) async-start(), calls=%async_computation.9 | async-start | bytes 4866048 | tf_op jit(solution)/shard_map/all_gather | solution.py:316
  141.0 92.7 %all-gather.15.cloned.1.call-start = ((), (), s32[]{:S(2)}) async-start(), calls=%async_computation.10 | async-start | bytes 1310720 | tf_op jit(solution)/shard_map/all_gather | solution.py:320
  241.6 29.8 %all-to-all-start.2 = ((bf16[4,128,1024]{2,1,0:T(8,128)(2,1)}), bf16[4,128,1024]{2,1,0:T(8,128)(2,1)}, u32[]{:S(2)}, u32[]{:S(2)}) async-start(bf16[4,128,1024]{2,1,0:T(8,128)(2,1)} %bitcast.213), calls=%async_computation.2 | async-start | bytes 2097152 | tf_op jit(solution)/shard_map/all_to_all | solution.py:280
  245.8 77.3 %all-gather.17.cloned.1.call-start = ((), (), s32[]{:S(2)}) async-start(), calls=%async_computation.11 | async-start | bytes 1310720 | tf_op jit(solution)/shard_map/all_gather | solution.py:365
  279.6 48.3 %all-to-all-start.1 = ((bf16[4,128,1024]{2,1,0:T(8,128)(2,1)}), bf16[4,128,1024]{2,1,0:T(8,128)(2,1)}, u32[]{:S(2)}, u32[]{:S(2)}) async-start(bf16[4,128,1024]{2,1,0:T(8,128)(2,1)} %bitcast.211), calls=%async_computation.1 | async-start | bytes 2097152 | tf_op jit(solution)/shard_map/all_to_all | solution.py:280
  327.9 55.1 %all-to-all-start.5 = ((bf16[8,128,2112]{1,2,0:T(8,128)(2,1)}), bf16[8,128,2112]{1,2,0:T(8,128)(2,1)}, u32[]{:S(2)}, u32[]{:S(2)}) async-start(bf16[8,128,2112]{1,2,0:T(8,128)(2,1)} %pad_maximum_fusion), calls=%async_computation.5 | async-start | bytes 8650752 | tf_op jit(solution)/shard_map/all_to_all | solution.py:280
  383.0 26.6 %all-to-all-start.3 = ((bf16[4,128,1024]{2,1,0:T(8,128)(2,1)}), bf16[4,128,1024]{2,1,0:T(8,128)(2,1)S(1)}, u32[]{:S(2)}, u32[]{:S(2)}) async-start(bf16[4,128,1024]{2,1,0:T(8,128)(2,1)} %bitcast.210), calls=%async_computation.3 | async-start | bytes 2097152 | tf_op jit(solution)/shard_map/all_to_all | solution.py:280
  409.6 92.9 %all-to-all-start.4 = ((bf16[8,128,1026]{1,2,0:T(8,128)(2,1)}), bf16[8,128,1026]{1,2,0:T(8,128)(2,1)}, u32[]{:S(2)}, u32[]{:S(2)}) async-start(bf16[8,128,1026]{1,2,0:T(8,128)(2,1)} %pad_maximum_fusion.1), calls=%async_computation.4 | async-start | bytes 4227072 | tf_op jit(solution)/shard_map/all_to_all | solution.py:280
  418.7 82.6 %copy-start.7 = (f32[128,1024]{1,0:T(8,128)S(1)}, f32[128,1024]{1,0:T(8,128)}, u32[]{:S(2)}) copy-start(f32[128,1024]{1,0:T(8,128)} %copy-done.6) | copy-start | bytes 1572868
  418.7 82.6 %copy-start.14 = (bf16[128,1024]{1,0:T(8,128)(2,1)S(1)}, bf16[128,1024]{1,0:T(8,128)(2,1)}, u32[]{:S(2)}) copy-start(bf16[128,1024]{1,0:T(8,128)(2,1)} %param.33) | copy-start | bytes 786436
  418.7 82.6 %copy-start.32 = (f32[1024]{0:T(1024)S(1)}, f32[1024]{0:T(1024)}, u32[]{:S(2)}) copy-start(f32[1024]{0:T(1024)} %param.29) | copy-start | bytes 12292
  418.8 82.6 %copy-start.57 = (f32[128]{0:T(128)S(1)}, f32[128]{0:T(128)}, u32[]{:S(2)}) copy-start(f32[128]{0:T(128)} %copy-done.55) | copy-start | bytes 1540
  418.8 82.6 %copy-start.64 = (f32[128]{0:T(128)S(1)}, f32[128]{0:T(128)}, u32[]{:S(2)}) copy-start(f32[128]{0:T(128)} %copy-done.63) | copy-start | bytes 1540
  (60 other events, 288.6 us)
Sparse Core Ops, SparseCore 0:
  10.3 30.5 all-gather.6
  43.4 28.3 all-gather.8
  139.1 26.0 all-gather.10
  167.0 37.2 all-gather.12
  205.7 27.9 all-gather.14
  276.2 46.9 all-gather.16
